TPU v7x, 128 devices: a whole 4x4x4 slice. The times are simulated.
128 devices in a mesh: row: 8 (over x_hi, y), col: 16 (over z, x_lo, core).
Axes of the slice: x: 4 (x_hi: 2, x_lo: 2; x = x_hi * 2 + x_lo), y: 4, z: 4, core: 2. Of those that a mesh axis runs over, the one named last changes fastest.
Arguments:
- pair_ints: bfloat16 [2048, 16384], P(None, ('row', 'col')), may hold values from -0.59765625 to 0.59765625
- denominators: float32 [2048], replicated, may hold values from 0.5 to 4
- lap_points: float32 [3], replicated, may hold values from 0.05 to 1.5
- lap_weights: float32 [3], replicated, may hold values from 0.2 to 1
Outputs:
- aux_matrices: float32 [3, 16384, 16384], P(None, 'row', 'col')
All inputs are finite; a program needn't handle non-finite values.
Results may differ from a plain program's by a relative error of at most 0.0027.
Values may be sent and summed in bfloat16 or wider, within the bound.
A program may use at most 128 MiB of HBM per device.

v0:
```python
import jax
import jax.numpy as jnp
from jax import lax
from jax.sharding import PartitionSpec as P


def on_device(pair_ints, denominators, lap_points, lap_weights):
    factors = lap_weights[:, None] * jnp.exp(-lap_points[:, None] * denominators[None, :])
    pair_rows = lax.all_to_all(pair_ints, ("row", "col"), split_axis=0, concat_axis=1, tiled=True)
    col_block = lax.all_to_all(pair_rows, "col", split_axis=1, concat_axis=0, tiled=True)
    col_whole = lax.all_gather(col_block, "row", axis=0, tiled=True)
    weighted = (
        lax.all_gather(pair_ints, "col", axis=1, tiled=True).astype(jnp.float32)[None]
        * factors[:, :, None]
    ).astype(jnp.bfloat16)
    return jnp.einsum("trp,rq->tpq", weighted, col_whole, preferred_element_type=jnp.float32)


def solution(mesh):
    in_specs = (P(None, ("row", "col")), P(), P(), P())
    out_specs = P(None, "row", "col")
    return jax.shard_map(
        on_device, mesh=mesh, in_specs=in_specs, out_specs=out_specs, check_vma=False
    )
```

profile of v0, /device:TPU:0, one launch (start us, length us, event | category | flops | bytes accessed | tf_op | source)
XLA Modules:
  0.0 196.7 jit_solution(1863049342206637796)
XLA Ops:
  6.5 0.0 all-gather.3.cloned.1.call-start
  6.5 0.7 all-gather.3.cloned.1.call-update
  7.3 0.0 all-gather.5.cloned.1.call-start
  7.3 28.6 %all_to_all.35 = bf16[128,16,128]{2,1,0:T(8,128)(2,1)S(1)} all-to-all(bf16[128,16,128]{2,1,0:T(8,128)(2,1)} %bitcast.8), channel_id=1, replica_groups=mesh['row'=8,'col'=16] {'row','col'}, dimensions={0} | all-to-all | bytes 1048576 | tf_op jit(solution)/shard_map/all_to_all | solution.py:9
  35.9 0.1 copy.10
  36.1 0.2 all_to_all.29
  36.3 0.3 copy.11
  36.6 18.0 %all_to_all.36 = bf16[16,16,1024]{2,0,1:T(8,128)(2,1)} all-to-all(bf16[16,16,1024]{2,0,1:T(8,128)(2,1)S(1)} %copy.11), channel_id=1, replica_groups=mesh['row'=8,'col'=16] {'col'}, dimensions={1} | all-to-all | bytes 1048576 | tf_op jit(solution)/shard_map/all_to_all | solution.py:10
  54.6 0.0 all-gather.5.cloned.1.call-update
  54.6 0.7 neg.4
  55.3 0.8 exponential_multiply_fusion
  56.1 27.6 %all-gather.3.cloned.1.call-done = bf16[2048,2048]{1,0:T(8,128)(2,1)} async-done(((bf16[2048,128]{1,0:T(8,128)(2,1)}), bf16[2048,2048]{1,0:T(8,128)(2,1)}) %all-gather.3.cloned.1.call-update) | async-done | bytes 8388624 | tf_op jit(solution)/shard_map/all_gather | solution.py:13
  83.7 13.1 %copy.9 = f32[2048,2048]{0,1:T(8,128)} copy(bf16[2048,2048]{1,0:T(8,128)(2,1)} %all-gather.3.cloned.1.call-done) | data formatting | bytes 25165824 | tf_op jit(solution)/shard_map/convert_element_type | solution.py:13
  96.8 59.4 %all-gather.5.cloned.1.call-done = bf16[2048,1024]{1,0:T(8,128)(2,1)} async-done(((bf16[256,1024]{1,0:T(8,128)(2,1)}), bf16[2048,1024]{1,0:T(8,128)(2,1)}) %all-gather.5.cloned.1.call-update) | async-done | bytes 4194320 | tf_op jit(solution)/shard_map/all_gather | solution.py:11
  156.3 33.6 %fusion = f32[3,2048,1024]{2,1,0:T(8,128)} fusion(f32[3,2048]{1,0:T(4,128)S(1)} %exponential_multiply_fusion, f32[2048,2048]{0,1:T(8,128)} %copy.9, bf16[2048,1024]{1,0:T(8,128)(2,1)} %all-gather.5.cloned.1.call-done), kind=kOutput, calls=%fused_computation.1 | convolution fusion | flops 25794969600 | bytes 46161920 | tf_op jit(solution)/shard_map/trp,rq->tpq/dot_general | solution.py:16
Async XLA Ops:
  6.5 77.2 %all-gather.3.cloned.1.call-start = ((), (), s32[]{:S(2)}) async-start(), calls=%async_computation.2 | async-start | bytes 8912896 | tf_op jit(solution)/shard_map/all_gather | solution.py:13
  7.3 149.0 %all-gather.5.cloned.1.call-start = ((), (), s32[]{:S(2)}) async-start(), calls=%async_computation.3 | async-start | bytes 4718592 | tf_op jit(solution)/shard_map/all_gather | solution.py:11
Sparse Core Ops, SparseCore 0:
  8.9 74.7 all-gather.2
  86.1 70.1 all-gather.4
where the time goes:
time: 197 us
  waiting for transfers between devices  87.8 us (45%)
  blocking collectives  46.6 us (24%)
  matrix products  33.6 us (17%)
  local copies, waits for them, and re-layouts  13.8 us (7%)
  between operations  13.4 us (7%)
    all_gather x1, waiting for transfers between devices, on_device(): col_whole = lax.all_gather(col_block, 'row', axis=0, tiled=True)  59.4 us
    dot_general x1, matrix products, on_device(): jnp.einsum('trp,rq->tpq', weighted, col_whole, preferred_element_type=jnp...  33.6 us
    all_to_all x1, blocking collectives, on_device(): lax.all_to_all(pair_ints, ('row', 'col'), split_axis=0, concat_axis=1, ti...  28.6 us
    all_gather x1, waiting for transfers between devices, on_device(): lax.all_gather(pair_ints, 'col', axis=1, tiled=True).astype(jnp.float32)  27.6 us
    all_to_all x1, blocking collectives, on_device(): lax.all_to_all(pair_rows, 'col', split_axis=1, concat_axis=0, tiled=True)  18 us
    convert_element_type x1, local copies, waits for them, and re-layouts, on_device(): lax.all_gather(pair_ints, 'col', axis=1, tiled=True).astype(jnp.float32)  13.1 us
  transfers between devices with their start and end apart: 2, of which 2 were waited for; matrix products, arithmetic and copies ran while one was open for 8% of the time, Pallas kernels for 0%

commit v1 on v0

--- a/solution.py
+++ b/solution.py
@@ -10,7 +10,7 @@
     col_block = lax.all_to_all(pair_rows, "col", split_axis=1, concat_axis=0, tiled=True)
     col_whole = lax.all_gather(col_block, "row", axis=0, tiled=True)
     weighted = (
-        lax.all_gather(pair_ints, "col", axis=1, tiled=True).astype(jnp.float32)[None]
+        jnp.concatenate(lax.all_gather(pair_ints, "col"), axis=1).astype(jnp.float32)[None]
         * factors[:, :, None]
     ).astype(jnp.bfloat16)
     return jnp.einsum("trp,rq->tpq", weighted, col_whole, preferred_element_type=jnp.float32)

time: 197 us -> 188 us (0.954)
  waiting for transfers between devices: 87.8 us -> 60.6 us
  other arithmetic: 1.45 us -> 12.7 us
  local copies, waits for them, and re-layouts: 13.8 us -> 18.4 us
  blocking collectives: 46.6 us -> 48.7 us
    all_gather x1, waiting for transfers between devices: 59.4 us -> 44.4 us  [on_device(): col_whole = lax.all_gather(col_block, 'row', axis=0, tiled=True)]
    all_gather x1, waiting for transfers between devices: 27.6 us -> 15.5 us  [on_device(): lax.all_gather(pair_ints, 'col')]
    convert_element_type x0 -> x1, other arithmetic: none -> 11.2 us  [on_device(): jnp.concatenate(lax.all_gather(pair_ints, 'col'), axis=1)]
    convert_element_type x1, local copies, waits for them, and re-layouts: 13.1 us -> 17.8 us  [on_device(): jnp.concatenate(lax.all_gather(pair_ints, 'col'), axis=1)]
    all_to_all x1, blocking collectives: 18 us -> 20.1 us  [on_device(): lax.all_to_all(pair_rows, 'col', split_axis=1, concat_axis=0, tiled=True)]
  transfers between devices with their start and end apart: 2 -> 2, of which waited for: 2 -> 2; matrix products, arithmetic and copies ran while one was open for 8% -> 16% of each run, Pallas kernels for 0% -> 0%
where the time goes in v1:
time: 188 us; the launch traced here: 187 us
  waiting for transfers between devices  60.6 us (32%)
  blocking collectives  48.7 us (26%)
  matrix products  33.6 us (18%)
  local copies, waits for them, and re-layouts  18.4 us (10%)
  between operations  13.4 us (7%)
  other arithmetic  12.7 us (7%)
    all_gather x1, waiting for transfers between devices, on_device(): col_whole = lax.all_gather(col_block, 'row', axis=0, tiled=True)  44.4 us
    dot_general x1, matrix products, on_device(): jnp.einsum('trp,rq->tpq', weighted, col_whole, preferred_element_type=jnp...  33.6 us
    all_to_all x1, blocking collectives, on_device(): lax.all_to_all(pair_ints, ('row', 'col'), split_axis=0, concat_axis=1, ti...  28.6 us
    all_to_all x1, blocking collectives, on_device(): lax.all_to_all(pair_rows, 'col', split_axis=1, concat_axis=0, tiled=True)  20.1 us
    convert_element_type x1, local copies, waits for them, and re-layouts, on_device(): jnp.concatenate(lax.all_gather(pair_ints, 'col'), axis=1)  17.8 us
    all_gather x1, waiting for transfers between devices, on_device(): lax.all_gather(pair_ints, 'col')  15.5 us
    convert_element_type x1, other arithmetic, on_device(): jnp.concatenate(lax.all_gather(pair_ints, 'col'), axis=1)  11.2 us
  transfers between devices with their start and end apart: 2, of which 2 were waited for; matrix products, arithmetic and copies ran while one was open for 16% of the time, Pallas kernels for 0%

profile of v1, /device:TPU:0, one launch (start us, length us, event | category | flops | bytes accessed | tf_op | source)
XLA Modules:
  0.0 187.5 jit_solution(7628359692394761362)
XLA Ops:
  6.5 0.0 all-gather.6.cloned.1.call-start
  6.5 0.7 all-gather.6.cloned.1.call-update
  7.3 0.0 all-gather.4.cloned.1.call-start
  7.3 28.6 %all_to_all.35 = bf16[128,16,128]{2,1,0:T(8,128)(2,1)S(1)} all-to-all(bf16[128,16,128]{2,1,0:T(8,128)(2,1)} %bitcast.15), channel_id=1, replica_groups=mesh['row'=8,'col'=16] {'row','col'}, dimensions={0} | all-to-all | bytes 1048576 | tf_op jit(solution)/shard_map/all_to_all | solution.py:9
  35.9 0.1 copy.11
  36.0 0.2 all_to_all.29
  36.2 0.3 copy.12
  36.5 20.1 %all_to_all.36 = bf16[16,16,1024]{2,0,1:T(8,128)(2,1)} all-to-all(bf16[16,16,1024]{2,0,1:T(8,128)(2,1)S(1)} %copy.12), channel_id=1, replica_groups=mesh['row'=8,'col'=16] {'col'}, dimensions={1} | all-to-all | bytes 1048576 | tf_op jit(solution)/shard_map/all_to_all | solution.py:10
  56.7 0.0 all-gather.4.cloned.1.call-update
  56.7 0.7 neg.4
  57.4 0.8 exponential_multiply_fusion
  58.2 15.5 %all-gather.6.cloned.1.call-done = bf16[32768,128]{1,0:T(8,128)(2,1)} async-done(((bf16[2048,128]{1,0:T(8,128)(2,1)}), bf16[32768,128]{1,0:T(8,128)(2,1)}) %all-gather.6.cloned.1.call-update) | async-done | bytes 8388624 | tf_op jit(solution)/shard_map/all_gather | solution.py:13
  73.6 11.2 %convert_bitcast_fusion = f32[2048,16,128]{2,0,1:T(8,128)} fusion(bf16[16,2048,128]{2,1,0:T(8,128)(2,1)} %bitcast.14), kind=kLoop, calls=%fused_computation.4 | loop fusion | flops 4194304 | bytes 25165824 | tf_op jit(solution)/shard_map/convert_element_type | solution.py:13
  84.9 17.8 %copy.10 = f32[2048,16,128]{0,2,1:T(8,128)} copy(f32[2048,16,128]{2,0,1:T(8,128)} %convert_bitcast_fusion) | data formatting | bytes 33554432 | tf_op jit(solution)/shard_map/convert_element_type | solution.py:13
  102.7 44.4 %all-gather.4.cloned.1.call-done = bf16[2048,1024]{1,0:T(8,128)(2,1)} async-done(((bf16[256,1024]{1,0:T(8,128)(2,1)}), bf16[2048,1024]{1,0:T(8,128)(2,1)}) %all-gather.4.cloned.1.call-update) | async-done | bytes 4194320 | tf_op jit(solution)/shard_map/all_gather | solution.py:11
  147.0 33.6 %fusion = f32[3,2048,1024]{2,1,0:T(8,128)} fusion(f32[3,2048]{1,0:T(4,128)S(1)} %exponential_multiply_fusion, f32[2048,2048]{0,1:T(8,128)} %bitcast.13, bf16[2048,1024]{1,0:T(8,128)(2,1)} %all-gather.4.cloned.1.call-done), kind=kOutput, calls=%fused_computation.1 | convolution fusion | flops 25794969600 | bytes 46161920 | tf_op jit(solution)/shard_map/trp,rq->tpq/dot_general | solution.py:16
Async XLA Ops:
  6.5 67.1 %all-gather.6.cloned.1.call-start = ((), (), s32[]{:S(2)}) async-start(), calls=%async_computation.3 | async-start | bytes 8912896 | tf_op jit(solution)/shard_map/all_gather | solution.py:13
  7.3 139.8 %all-gather.4.cloned.1.call-start = ((), (), s32[]{:S(2)}) async-start(), calls=%async_computation.2 | async-start | bytes 4718592 | tf_op jit(solution)/shard_map/all_gather | solution.py:11
Sparse Core Ops, SparseCore 0:
  9.0 64.5 all-gather.5
  76.0 70.9 all-gather.3
